TPU v7x, 512 devices: a whole 4x4x16 slice. The times are simulated.
512 devices in a mesh: dp: 16 (over x, y), expert: 32 (over z, core).
Axes of the slice: x: 4, y: 4, z: 16, core: 2. Of those that a mesh axis runs over, the one named last changes fastest.
Arguments:
- tokens: bfloat16 [8192, 1024], P(('dp', 'expert')), may hold values from -6 to 6
- upstream: bfloat16 [8192, 1024], P(('dp', 'expert')), may hold values from -6 to 6
- expert_ids: int32 [8192, 8], P(('dp', 'expert')), may hold values from 0 to 127, all different within a row; in each aligned block of 16 rows (0 to 15, 16 to 31, ...) at most 2 rows name the same one
- gates: float32 [8192, 8], P(('dp', 'expert')), may hold values from 0.05 to 1
- relocate: int32 [32, 4], replicated, may hold values from 0 to 1, as said below
- w_gate_up: bfloat16 [32, 16, 384, 1024], P('expert', 'dp'), may hold values from -0.1875 to 0.1875
- w_down: bfloat16 [32, 16, 192, 1024], P('expert', 'dp'), may hold values from -0.21875 to 0.21875
Outputs:
- grad_tokens: bfloat16 [8192, 1024], P(('dp', 'expert'))
- grad_gate_up: bfloat16 [32, 16, 384, 1024], P('expert', 'dp')
- grad_down: bfloat16 [32, 16, 192, 1024], P('expert', 'dp')
Inputs may be any that keep to these rules, and one draw needn't show every extreme that they name: `expert_ids`: each row names 8 different experts; the rows of one device name one expert at most 2 times, and some device reaches 2. `relocate`: the first and the second half of the rows are equal; both values occur.
All inputs are finite; a program needn't handle non-finite values.
Results may differ from a plain program's by a relative error of at most 0.0064.
Values may be sent and summed in bfloat16 or wider, within the bound.
A program may use at most 64 MiB of HBM per device.

v0:
```python
import jax
import jax.numpy as jnp
from jax import lax
from jax.sharding import PartitionSpec as P

SLICES = 4
CAP = 2
contract_last = (((1,), (1,)), ((), ()))
contract_first = (((0,), (0,)), ((), ()))


def silu_parts(values_in):
    sigmoid_of = jax.nn.sigmoid(values_in)
    return (values_in * sigmoid_of, sigmoid_of * (1.0 + values_in * (1.0 - sigmoid_of)))


def half_swap(block, count, parity):
    half = count // 2
    route = [(c, (c + half) % count) for c in range(count) if c % 2 == parity]
    return lax.ppermute(block, "expert", route)


def three_parts(gates):
    first = lax.reduce_precision(gates, 8, 7)
    rest = gates - first
    second = lax.reduce_precision(rest, 8, 7)
    third = rest - second
    return [part.astype(jnp.bfloat16) for part in (first, second, third)]


def block_rank(hits, tok_dev):
    grouped = hits.reshape(hits.shape[0], -1, tok_dev)
    earlier = jnp.arange(tok_dev)[:, None] > jnp.arange(tok_dev)[None, :]
    ranks = jnp.sum(jnp.where(earlier[None, None], grouped[:, :, None, :], 0), axis=-1)
    return ranks.reshape(hits.shape)


def per_device(tokens, upstream, expert_ids, gates, relocate, w_gate_up, w_down):
    n_rows = lax.axis_size("dp")
    n_cols = lax.axis_size("expert")
    slots = n_rows // SLICES
    experts = slots * n_cols
    tok_dev, width = tokens.shape
    top = expert_ids.shape[1]
    slice_width = w_down.shape[2]
    half = n_cols // 2
    col = lax.axis_index("expert")
    slot_here = lax.axis_index("dp") // SLICES
    y_groups = [[x * SLICES + y for y in range(SLICES)] for x in range(slots)]
    x_groups = [[x * SLICES + y for x in range(slots)] for y in range(SLICES)]
    own_pack = jnp.concatenate([w_gate_up[0, 0], w_down[0, 0]], axis=0)
    far_pack = half_swap(own_pack, n_cols, 0)
    meta = jnp.concatenate(
        [expert_ids.astype(jnp.bfloat16)]
        + three_parts(gates)
        + [jnp.zeros((tok_dev, 128 - 4 * top), jnp.bfloat16)],
        axis=1,
    )
    packed = jnp.concatenate([tokens, upstream, meta], axis=1)
    gathered = lax.all_gather(packed, "expert", axis=0, tiled=True)
    even = col % 2 == 0
    rel_row = jnp.sum(jnp.where(jnp.arange(n_cols)[:, None] == col, relocate, 0), axis=0)
    served = jnp.where(even, (col + half * rel_row) % n_cols, col) * slots + jnp.arange(slots)
    meta_all = gathered[:, 2 * width :].astype(jnp.float32)
    ids_all = meta_all[:, :top].astype(jnp.int32)
    gates_all = (
        meta_all[:, top : 2 * top] + meta_all[:, 2 * top : 3 * top] + meta_all[:, 3 * top : 4 * top]
    )
    match = ids_all[None] == served[:, None, None]
    hits = jnp.sum(match.astype(jnp.int32), axis=-1)
    gate_of = jnp.sum(jnp.where(match, gates_all[None], 0.0), axis=-1)
    n_tok = ids_all.shape[0]
    place = CAP * (jnp.arange(n_tok, dtype=jnp.int32) // tok_dev)[None] + block_rank(hits, tok_dev)
    seats = n_cols * CAP
    seat = (hits[:, None, :] > 0) & (
        place[:, None, :] == jnp.arange(seats, dtype=jnp.int32)[None, :, None]
    )
    select = seat.reshape(slots * seats, n_tok).astype(jnp.bfloat16)
    rows = jnp.dot(select, gathered[:, : 2 * width], preferred_element_type=jnp.float32)
    gate_rows = jnp.sum(jnp.where(seat, gate_of[:, None, :], 0.0), axis=-1).reshape(-1, 1)
    sent = jnp.concatenate(
        [rows[:, :width].astype(jnp.bfloat16), (gate_rows * rows[:, width:]).astype(jnp.bfloat16)],
        axis=1,
    )
    at_x = lax.all_to_all(
        sent, "dp", split_axis=0, concat_axis=0, axis_index_groups=x_groups, tiled=True
    )
    all_rows = lax.all_gather(at_x, "dp", axis=0, axis_index_groups=y_groups, tiled=True)
    rows_x = all_rows[:, :width]
    rows_d = all_rows[:, width:]
    rel_here = jnp.sum(jnp.where(jnp.arange(slots) == slot_here, rel_row, 0))
    pack = jnp.where(even & (rel_here == 1), far_pack, own_pack)
    gate_up = pack[: 2 * slice_width]
    down_rows = pack[2 * slice_width :]
    gate_and_up = lax.dot_general(
        rows_x, gate_up, contract_last, preferred_element_type=jnp.float32
    )
    gate_pre = gate_and_up[:, :slice_width]
    up_pre = gate_and_up[:, slice_width:]
    activated, slope_of = silu_parts(gate_pre)
    hidden = (activated * up_pre).astype(jnp.bfloat16)
    hidden_grad = lax.dot_general(
        rows_d, down_rows, contract_last, preferred_element_type=jnp.float32
    )
    pre_grads = jnp.concatenate(
        [
            (hidden_grad * up_pre * slope_of).astype(jnp.bfloat16),
            (hidden_grad * activated).astype(jnp.bfloat16),
        ],
        axis=1,
    )
    slice_part = jnp.dot(pre_grads, gate_up, preferred_element_type=jnp.float32).astype(
        jnp.bfloat16
    )
    grad_gu = lax.dot_general(
        pre_grads, rows_x, contract_first, preferred_element_type=jnp.float32
    ).astype(jnp.bfloat16)
    grad_dn = lax.dot_general(
        hidden, rows_d, contract_first, preferred_element_type=jnp.float32
    ).astype(jnp.bfloat16)
    grad_pack = jnp.concatenate([grad_gu, grad_dn], axis=0)
    far_grads = half_swap(grad_pack, n_cols, 1)
    grad_pack = jnp.where(~even & (rel_here == 1), far_grads, grad_pack)
    parts = lax.all_to_all(
        slice_part, "dp", split_axis=0, concat_axis=0, axis_index_groups=y_groups, tiled=True
    )
    summed = jnp.sum(
        parts.reshape(SLICES, slots * seats, width).astype(jnp.float32), axis=0
    ).astype(jnp.bfloat16)
    back = lax.all_to_all(
        summed, "dp", split_axis=0, concat_axis=0, axis_index_groups=x_groups, tiled=True
    )
    partial = lax.dot_general(select, back, contract_first, preferred_element_type=jnp.float32)
    grad_tokens = lax.psum_scatter(partial, "expert", scatter_dimension=0, tiled=True).astype(
        jnp.bfloat16
    )
    return (
        grad_tokens,
        grad_pack[: 2 * slice_width].reshape(w_gate_up.shape),
        grad_pack[2 * slice_width :].reshape(w_down.shape),
    )


def solution(mesh):
    return jax.shard_map(
        per_device,
        mesh=mesh,
        in_specs=(
            P(("dp", "expert"), None),
            P(("dp", "expert"), None),
            P(("dp", "expert"), None),
            P(("dp", "expert"), None),
            P(),
            P("expert", "dp", None, None),
            P("expert", "dp", None, None),
        ),
        out_specs=(
            P(("dp", "expert"), None),
            P("expert", "dp", None, None),
            P("expert", "dp", None, None),
        ),
        check_vma=False,
    )
```

profile of v0, /device:TPU:28, one launch (start us, length us, event | category | flops | bytes accessed | tf_op | source)
XLA Modules:
  0.0 352.9 jit_solution(1204173419493060899)
XLA Ops:
  7.2 0.8 copy.30
  8.0 0.8 copy.31
  8.7 1.5 concatenate.15
  10.4 0.8 select_reduce_fusion.2
  11.2 0.6 iota_add_fusion
  11.9 74.4 %all-gather.3.cloned.1.call-done = bf16[512,2176]{1,0:T(8,128)(2,1)} async-done(((bf16[16,2176]{1,0:T(8,128)(2,1)}), bf16[512,2176]{1,0:T(8,128)(2,1)}) %all-gather.3.cloned.1.call-update) | async-done | bytes 2228240 | tf_op jit(solution)/shard_map/all_gather | solution.py:60
  86.3 0.9 slice.65
  88.6 2.3 fusion
  91.2 17.6 %all_to_all.30 = bf16[4,64,2048]{2,1,0:T(8,128)(2,1)} all-to-all(bf16[4,64,2048]{2,1,0:T(8,128)(2,1)S(1)} %bitcast.21), channel_id=1, replica_groups={{0,128,256,384},{32,160,288,416},{64,192,320,448},{96,224,352,480},{1,1..., dimensions={0} | all-to-all | bytes 2097152 | tf_op jit(solution)/shard_map/all_to_all | solution.py:85
  109.0 8.5 %collective-permute-start = (bf16[576,1024]{1,0:T(8,128)(2,1)S(1)}, bf16[576,1024]{1,0:T(8,128)(2,1)S(1)}, u32[]{:S(2)}, u32[]{:S(2)}) collective-permute-start(bf16[576,1024]{1,0:T(8,128)(2,1)S(1)} %pad_maximum_fusion), channel_id=1, source_target_pairs={{0,16},{2,18},{4,20},{6,22},{8,24},{10,26},{12,28},{14,30},{16,0},... | collective-permute-start | bytes 3538952 | tf_op jit(solution)/shard_map/ppermute | solution.py:20
  118.2 44.6 %collective-permute-done = bf16[576,1024]{1,0:T(8,128)(2,1)S(1)} collective-permute-done((bf16[576,1024]{1,0:T(8,128)(2,1)S(1)}, bf16[576,1024]{1,0:T(8,128)(2,1)S(1)}, u32[]{:S(2)}, u32[]{:S(2)}) %collective-permute-start) | collective-permute-done | bytes 1179680 | tf_op jit(solution)/shard_map/ppermute | solution.py:20
  163.3 2.8 fusion.4
  166.1 1.0 multiply_convert_fusion.2
  167.3 1.3 convolution_convert_fusion
  168.6 26.8 %all_to_all.31 = bf16[4,256,1024]{2,1,0:T(8,128)(2,1)S(1)} all-to-all(bf16[4,256,1024]{2,1,0:T(8,128)(2,1)S(1)} %bitcast.24), channel_id=1, replica_groups={{0,32,64,96},{128,160,192,224},{256,288,320,352},{384,416,448,480},{1,3..., dimensions={0} | all-to-all | bytes 4194304 | tf_op jit(solution)/shard_map/all_to_all | solution.py:124
  195.8 10.0 %all_to_all.32 = bf16[4,64,1024]{2,1,0:T(8,128)(2,1)S(1)} all-to-all(bf16[4,64,1024]{2,1,0:T(8,128)(2,1)S(1)} %bitcast.25), channel_id=1, replica_groups={{0,128,256,384},{32,160,288,416},{64,192,320,448},{96,224,352,480},{1,1..., dimensions={0} | all-to-all | bytes 1048576 | tf_op jit(solution)/shard_map/all_to_all | solution.py:130
  205.7 1.8 convolution_bitcast_fusion
  207.6 2.7 fusion.10
  210.9 0.6 fusion.13
  211.6 0.7 collective-permute-start.1
  212.9 0.8 slice_bitcast_fusion.1
  213.6 0.9 slice_bitcast_fusion
  214.6 130.4 %reduce-scatter.2.cloned.1.call-done = f32[16,1024]{1,0:T(8,128)} async-done(((f32[512,1024]{1,0:T(8,128)}), f32[16,1024]{1,0:T(8,128)}) %reduce-scatter.2.cloned.1.call-update) | async-done | bytes 65552 | tf_op jit(solution)/shard_map/reduce_scatter | solution.py:134
  344.9 1.5 convert_element_type.60
  (51 shorter events, 4.2 us)
Async XLA Ops:
  7.2 79.2 %all-gather.3.cloned.1.call-start = ((), (), s32[]{:S(2)}) async-start(), calls=%async_computation.4 | async-start | bytes 2297856 | tf_op jit(solution)/shard_map/all_gather | solution.py:60
  10.3 153.0 %all-gather.5.cloned.1.call-start = ((), (), s32[]{:S(2)}) async-start(), calls=%async_computation.5 | async-start | bytes 5242880 | tf_op jit(solution)/shard_map/all_gather | solution.py:88
  91.2 17.7 %copy-start = (bf16[1,1,384,1024]{3,2,1,0:T(8,128)(2,1)S(1)}, bf16[1,1,384,1024]{3,2,1,0:T(8,128)(2,1)}, u32[]{:S(2)}) copy-start(bf16[1,1,384,1024]{3,2,1,0:T(8,128)(2,1)} %param.12) | copy-start | bytes 2359300
  91.2 17.7 %copy-start.1 = (bf16[1,1,192,1024]{3,2,1,0:T(8,128)(2,1)S(1)}, bf16[1,1,192,1024]{3,2,1,0:T(8,128)(2,1)}, u32[]{:S(2)}) copy-start(bf16[1,1,192,1024]{3,2,1,0:T(8,128)(2,1)} %param.13) | copy-start | bytes 1179652
  108.9 236.1 %reduce-scatter.2.cloned.1.call-start = ((), (), s32[]{:S(2)}) async-start(), calls=%async_computation.6 | async-start | bytes 2162688 | tf_op jit(solution)/shard_map/reduce_scatter | solution.py:134
  109.0 53.8 %collective-permute-start = (bf16[576,1024]{1,0:T(8,128)(2,1)S(1)}, bf16[576,1024]{1,0:T(8,128)(2,1)S(1)}, u32[]{:S(2)}, u32[]{:S(2)}) collective-permute-start(bf16[576,1024]{1,0:T(8,128)(2,1)S(1)} %pad_maximum_fusion), channel_id=1, source_target_pairs={{0,16},{2,18},{4,20},{6,22},{8,24},{10,26},{12,28},{14,30},{16,0},... | collective-permute-start | bytes 3538952 | tf_op jit(solution)/shard_map/ppermute | solution.py:20
  163.3 2.8 copy-start.2
  166.1 1.1 copy-start.4
  207.6 2.8 copy-start.3
  207.6 3.3 copy-start.5
  211.6 0.8 collective-permute-start.1
Sparse Core Ops, SparseCore 0:
  10.7 75.6 all-gather.2
  109.0 51.6 all-gather.4
  207.7 137.2 reduce-scatter.1
where the time goes:
time: 353 us
  waiting for transfers between devices  249 us (71%)
  blocking collectives  54.3 us (15%)
  between operations  14.7 us (4%)
  matrix products  12.6 us (4%)
  starting transfers between devices  9.4 us (3%)
  local copies, waits for them, and re-layouts  7.02 us (2%)
  other arithmetic  5.47 us (2%)
    reduce_scatter x1, waiting for transfers between devices, per_device(): lax.psum_scatter(partial, 'expert', scatter_dimension=0, tiled=True)  130 us
    all_gather x1, waiting for transfers between devices, per_device(): gathered = lax.all_gather(packed, 'expert', axis=0, tiled=True)  74.4 us
    ppermute x2, waiting for transfers between devices, half_swap(): return lax.ppermute(block, 'expert', route)  44.6 us
    all_to_all x1, blocking collectives, per_device(): lax.all_to_all(slice_part, 'dp', split_axis=0, concat_axis=0, axis_index_...  26.8 us
    all_to_all x1, blocking collectives, per_device(): lax.all_to_all(sent, 'dp', split_axis=0, concat_axis=0, axis_index_groups...  17.6 us
    all_to_all x1, blocking collectives, per_device(): lax.all_to_all(summed, 'dp', split_axis=0, concat_axis=0, axis_index_grou...  9.97 us
    ppermute x2, starting transfers between devices, half_swap(): return lax.ppermute(block, 'expert', route)  9.28 us
  transfers between devices with their start and end apart: 5, of which 3 were waited for; matrix products, arithmetic and copies ran while one was open for 2% of the time, Pallas kernels for 0%

commit v1 on v0

--- a/solution.py
+++ b/solution.py
@@ -57,7 +57,9 @@
         axis=1,
     )
     packed = jnp.concatenate([tokens, upstream, meta], axis=1)
-    gathered = lax.all_gather(packed, "expert", axis=0, tiled=True)
+    gathered = jnp.concatenate(
+        lax.all_to_all(jnp.stack([packed] * lax.axis_size("expert")), "expert", 0, 0), axis=0
+    )
     even = col % 2 == 0
     rel_row = jnp.sum(jnp.where(jnp.arange(n_cols)[:, None] == col, relocate, 0), axis=0)
     served = jnp.where(even, (col + half * rel_row) % n_cols, col) * slots + jnp.arange(slots)

time: 353 us -> 400 us (1.13)
  the two profiles are of different devices: /device:TPU:28 before, /device:TPU:2 now
where the time goes in v1:
time: 400 us; the launch traced here: 399 us
  waiting for transfers between devices  291 us (73%)
  blocking collectives  50.6 us (13%)
  starting transfers between devices  19.6 us (5%)
  between operations  15 us (4%)
  matrix products  11 us (3%)
  other arithmetic  6.12 us (2%)
  local copies, waits for them, and re-layouts  5.86 us (1%)
    reduce_scatter x1, waiting for transfers between devices, per_device(): lax.psum_scatter(partial, 'expert', scatter_dimension=0, tiled=True)  135 us
    all_to_all x1, waiting for transfers between devices, per_device(): lax.all_to_all(jnp.stack([packed] * lax.axis_size('expert')), 'expert', 0...  103 us
    ppermute x2, waiting for transfers between devices, half_swap(): return lax.ppermute(block, 'expert', route)  53.1 us
    all_to_all x1, blocking collectives, per_device(): lax.all_to_all(slice_part, 'dp', split_axis=0, concat_axis=0, axis_index_...  21.2 us
    all_to_all x1, blocking collectives, per_device(): lax.all_to_all(sent, 'dp', split_axis=0, concat_axis=0, axis_index_groups...  18.2 us
    all_to_all x1, starting transfers between devices, per_device(): lax.all_to_all(jnp.stack([packed] * lax.axis_size('expert')), 'expert', 0...  15.6 us
    all_to_all x1, blocking collectives, per_device(): lax.all_to_all(summed, 'dp', split_axis=0, concat_axis=0, axis_index_grou...  11.2 us
  transfers between devices with their start and end apart: 5, of which 3 were waited for; matrix products, arithmetic and copies ran while one was open for 2% of the time, Pallas kernels for 0%

profile of v1, /device:TPU:2, one launch (start us, length us, event | category | flops | bytes accessed | tf_op | source)
XLA Modules:
  0.0 399.5 jit_solution(15823126766946920039)
XLA Ops:
  7.2 0.7 convert_element_type.49
  7.9 0.7 fusion.29
  8.9 0.9 concatenate.15
  9.8 1.5 stack.2
  11.3 15.6 %all-to-all-start = ((bf16[32,16,2176]{2,1,0:T(8,128)(2,1)}), bf16[32,16,2176]{2,1,0:T(8,128)(2,1)S(1)}, u32[]{:S(2)}, u32[]{:S(2)}) async-start(bf16[32,16,2176]{2,1,0:T(8,128)(2,1)} %stack.2), calls=%async_computation | async-start | bytes 4456448 | tf_op jit(solution)/shard_map/all_to_all | solution.py:61
  27.2 0.6 iota_add_fusion
  27.9 103.4 %all-to-all-done = bf16[32,16,2176]{2,1,0:T(8,128)(2,1)S(1)} async-done(((bf16[32,16,2176]{2,1,0:T(8,128)(2,1)}), bf16[32,16,2176]{2,1,0:T(8,128)(2,1)S(1)}, u32[]{:S(2)}, u32[]{:S(2)}) %all-to-all-start) | async-done | bytes 2228256 | tf_op jit(solution)/shard_map/all_to_all | solution.py:61
  132.6 0.7 fusion
  133.6 18.2 %all_to_all.35 = bf16[4,64,2048]{2,1,0:T(8,128)(2,1)} all-to-all(bf16[4,64,2048]{2,1,0:T(8,128)(2,1)S(1)} %bitcast.24), channel_id=1, replica_groups={{0,128,256,384},{32,160,288,416},{64,192,320,448},{96,224,352,480},{1,1..., dimensions={0} | all-to-all | bytes 2097152 | tf_op jit(solution)/shard_map/all_to_all | solution.py:87
  152.0 3.2 collective-permute-start
  155.9 53.1 %collective-permute-done = bf16[576,1024]{1,0:T(8,128)(2,1)S(1)} collective-permute-done((bf16[576,1024]{1,0:T(8,128)(2,1)S(1)}, bf16[576,1024]{1,0:T(8,128)(2,1)S(1)}, u32[]{:S(2)}, u32[]{:S(2)}) %collective-permute-start) | collective-permute-done | bytes 1179680 | tf_op jit(solution)/shard_map/ppermute | solution.py:20
  209.4 2.7 fusion.4
  212.3 1.1 multiply_convert_fusion.2
  213.4 1.3 convolution_convert_fusion
  214.7 21.2 %all_to_all.36 = bf16[4,256,1024]{2,1,0:T(8,128)(2,1)S(1)} all-to-all(bf16[4,256,1024]{2,1,0:T(8,128)(2,1)S(1)} %bitcast.27), channel_id=1, replica_groups={{0,32,64,96},{128,160,192,224},{256,288,320,352},{384,416,448,480},{1,3..., dimensions={0} | all-to-all | bytes 4194304 | tf_op jit(solution)/shard_map/all_to_all | solution.py:126
  236.3 11.2 %all_to_all.37 = bf16[4,64,1024]{2,1,0:T(8,128)(2,1)S(1)} all-to-all(bf16[4,64,1024]{2,1,0:T(8,128)(2,1)S(1)} %bitcast.28), channel_id=1, replica_groups={{0,128,256,384},{32,160,288,416},{64,192,320,448},{96,224,352,480},{1,1..., dimensions={0} | all-to-all | bytes 1048576 | tf_op jit(solution)/shard_map/all_to_all | solution.py:132
  247.6 1.8 convolution_bitcast_fusion
  249.4 2.7 fusion.10
  252.7 0.6 fusion.13
  253.4 0.7 collective-permute-start.1
  254.7 0.8 slice_bitcast_fusion.1
  255.5 0.9 slice_bitcast_fusion
  256.4 134.8 %reduce-scatter.2.cloned.1.call-done = f32[16,1024]{1,0:T(8,128)} async-done(((f32[512,1024]{1,0:T(8,128)}), f32[16,1024]{1,0:T(8,128)}) %reduce-scatter.2.cloned.1.call-update) | async-done | bytes 65552 | tf_op jit(solution)/shard_map/reduce_scatter | solution.py:136
  391.2 1.5 convert_element_type.60
  (55 shorter events, 4.5 us)
Async XLA Ops:
  11.3 15.8 %copy-start.2 = (s32[32,4]{0,1:T(4,128)S(1)}, s32[32,4]{0,1:T(4,128)}, u32[]{:S(2)}) copy-start(s32[32,4]{0,1:T(4,128)} %param.11) | copy-start | bytes 1540
  11.3 119.9 %all-to-all-start = ((bf16[32,16,2176]{2,1,0:T(8,128)(2,1)}), bf16[32,16,2176]{2,1,0:T(8,128)(2,1)S(1)}, u32[]{:S(2)}, u32[]{:S(2)}) async-start(bf16[32,16,2176]{2,1,0:T(8,128)(2,1)} %stack.2), calls=%async_computation | async-start | bytes 4456448 | tf_op jit(solution)/shard_map/all_to_all | solution.py:61
  26.9 182.5 %all-gather.2.cloned.1.call-start = ((), (), s32[]{:S(2)}) async-start(), calls=%async_computation.5 | async-start | bytes 5242880 | tf_op jit(solution)/shard_map/all_gather | solution.py:90
  133.6 18.3 %copy-start = (bf16[1,1,384,1024]{3,2,1,0:T(8,128)(2,1)S(1)}, bf16[1,1,384,1024]{3,2,1,0:T(8,128)(2,1)}, u32[]{:S(2)}) copy-start(bf16[1,1,384,1024]{3,2,1,0:T(8,128)(2,1)} %param.12) | copy-start | bytes 2359300
  133.6 18.3 %copy-start.1 = (bf16[1,1,192,1024]{3,2,1,0:T(8,128)(2,1)S(1)}, bf16[1,1,192,1024]{3,2,1,0:T(8,128)(2,1)}, u32[]{:S(2)}) copy-start(bf16[1,1,192,1024]{3,2,1,0:T(8,128)(2,1)} %param.13) | copy-start | bytes 1179652
  151.9 239.3 %reduce-scatter.2.cloned.1.call-start = ((), (), s32[]{:S(2)}) async-start(), calls=%async_computation.6 | async-start | bytes 2162688 | tf_op jit(solution)/shard_map/reduce_scatter | solution.py:136
  152.0 56.9 %collective-permute-start = (bf16[576,1024]{1,0:T(8,128)(2,1)S(1)}, bf16[576,1024]{1,0:T(8,128)(2,1)S(1)}, u32[]{:S(2)}, u32[]{:S(2)}) collective-permute-start(bf16[576,1024]{1,0:T(8,128)(2,1)S(1)} %pad_maximum_fusion), channel_id=1, source_target_pairs={{0,16},{2,18},{4,20},{6,22},{8,24},{10,26},{12,28},{14,30},{16,0},... | collective-permute-start | bytes 3538952 | tf_op jit(solution)/shard_map/ppermute | solution.py:20
  209.4 2.8 copy-start.3
  212.3 1.1 copy-start.5
  249.4 2.8 copy-start.4
  249.4 3.3 copy-start.6
  253.4 0.8 collective-permute-start.1
Sparse Core Ops, SparseCore 0:
  152.0 49.2 all-gather.1
  249.5 141.6 reduce-scatter.1
